TPU v7x, 128 devices: a whole 4x4x4 slice. The times are simulated.
128 devices in a mesh: head: 8 (over x_lo, z), ctx: 16 (over y, x_hi, core).
Axes of the slice: x: 4 (x_hi: 2, x_lo: 2; x = x_hi * 2 + x_lo), y: 4, z: 4, core: 2. Of those that a mesh axis runs over, the one named last changes fastest.
Arguments:
- queries: bfloat16 [2, 8192, 4096], P(None, 'ctx', 'head'), may hold values from -20 to 20
- keys: bfloat16 [2, 8192, 4096], P(None, 'ctx', 'head'), may hold values from -20 to 20
- values: bfloat16 [2, 8192, 4096], P(None, 'ctx', 'head'), may hold values from -6 to 6
- token_rates: float32 [2, 8192, 8], P(None, 'ctx', 'head'), may hold values from 0.05 to 1
- fast_init: float32 [3, 8, 512, 512], P(None, 'head'), may hold values from -0.25 to 0.25
- out_gain: float32 [4096], P('head'), may hold values from 0.5 to 1.5
- out_weight: bfloat16 [4096, 4096], P('head'), may hold values from -0.09375 to 0.09375
Outputs:
- layer_out: bfloat16 [2, 8192, 4096], P(None, ('ctx', 'head'))
- fast_final: float32 [3, 8, 512, 512], P(None, 'head')
All inputs are finite; a program needn't handle non-finite values.
Results may differ from a plain program's by a relative error of at most 0.022.
Values may be sent and summed in bfloat16 or wider, within the bound.
A program may use at most 128 MiB of HBM per device.

v0:
```python
import functools

import jax
import jax.numpy as jnp
from jax import lax
from jax.experimental import pallas as pl
from jax.experimental.pallas import tpu as pltpu
from jax.sharding import PartitionSpec as P

AH = 128
NS_ITERS = 2
coef_a = 3.4445
coef_b = -4.775
coef_c = 2.0315
F32 = jnp.float32
BF = jnp.bfloat16


def dot_nn(a, b):
    return lax.dot_general(a, b, (((1,), (0,)), ((), ())), preferred_element_type=F32)


def dot_tn(a, b):
    return lax.dot_general(a, b, (((0,), (0,)), ((), ())), preferred_element_type=F32)


def dot_nt(a, b):
    return lax.dot_general(a, b, (((1,), (1,)), ((), ())), preferred_element_type=F32)


def normed(x):
    return x * lax.rsqrt(jnp.mean(x * x, axis=-1, keepdims=True) + 1e-06)


def kernel(
    q_hbm, k_hbm, v_hbm, rates, w_hbm, gain, wout,
    out, fin,
    qv, kv, win, state, wb, gs, ga, g1, gb, g2, gc, xg, acc, mrow, lrow, fo, mixed, mz, wz, pp, pr,
    load_sem, ysnd, yrcv, xsnd, xrcv, c1snd, c1rcv, c3snd, c3rcv,
    asnd, arcv, bsnd, brcv, csnd, crcv, dsnd, drcv, esnd, ercv, fsnd, frcv,
    wsnd, wrcv, wfsnd, wfrcv, wcsnd, wcrcv, zsnd, zrcv, osnd, orcv,
):
    head = lax.axis_index("head")
    ctx = lax.axis_index("ctx")
    xlo, z = head // 4, head % 4
    y, xhi, core = ctx // 4, (ctx // 2) % 2, ctx % 2
    other = {"head": head, "ctx": ctx + 1 - 2 * core}
    across = {"head": head, "ctx": ctx + 2 - 4 * xhi}
    along = [{"head": head, "ctx": (ctx + 4 * r) % 16} for r in (1, 2, 3)]
    up = [{"head": xlo * 4 + (z + r) % 4, "ctx": ctx} for r in (1, 2, 3)]
    beside = {"head": (head + 4) % 8, "ctx": ctx}

    def remote(src, dst, snd, rcv, device):
        return pltpu.make_async_remote_copy(
            src_ref=src, dst_ref=dst, send_sem=snd, recv_sem=rcv,
            device_id=device, device_id_type=pl.DeviceIdType.MESH,
        )

    loads = [
        pltpu.make_async_copy(k_hbm, kv.at[0], load_sem.at[0]),
        pltpu.make_async_copy(v_hbm, kv.at[1], load_sem.at[1]),
        pltpu.make_async_copy(w_hbm, state, load_sem.at[2]),
        pltpu.make_async_copy(q_hbm, qv, load_sem.at[3]),
        pltpu.make_async_copy(wout, wz.at[z], load_sem.at[4]),
    ]
    for load in loads[:4]:
        load.start()

    barrier = pltpu.get_barrier_semaphore()
    partners = [other, across, beside] + along + up
    for partner in partners:
        pl.semaphore_signal(barrier, 1, device_id=partner, device_id_type=pl.DeviceIdType.MESH)
    pl.semaphore_wait(barrier, len(partners))

    own_kv = (k_hbm, v_hbm)

    def y_copy(i):
        s, w = i // 2, i % 2
        return remote(own_kv[w].at[s], win.at[3, w, s], ysnd.at[i], yrcv.at[i], along[0])

    def x_copy(i, forward):
        s, w = i // 2, i % 2
        src = win.at[3, w, s] if forward else own_kv[w].at[s]
        return remote(src, win.at[1, w, s], xsnd.at[i], xrcv.at[i], across)

    def c1_copy(i, forward):
        s, w = i // 2, i % 2
        src = win.at[1, w, s] if forward else own_kv[w].at[s]
        return remote(src, win.at[0, w, s], c1snd.at[i], c1rcv.at[i], other)

    def c3_copy(i, slot):
        s, w = i // 2, i % 2
        return remote(win.at[slot, w, s], win.at[2, w, s], c3snd.at[i], c3rcv.at[i], other)

    def x_own(i):
        @pl.when(xhi == 0)
        def _():
            x_copy(i, False).start()

    def got_y(i):
        y_copy(i).wait_recv()

        @pl.when(xhi == 1)
        def _():
            x_copy(i, True).start()

        @pl.when(core == 1)
        def _():
            c3_copy(i, 3).start()

    def got_x(i):
        x_copy(i, False).wait_recv()

        @pl.when(core == 0)
        def _():
            c3_copy(i, 1).start()

        @pl.when(core == 1)
        def _():
            c1_copy(i, True).start()

    def w_cols(piece):
        return pl.ds(pl.multiple_of(core * 2048 + piece * 1024, 1024), 1024)

    half_cols = pl.ds(pl.multiple_of(core * 2048, 2048), 2048)

    def w_copy(direction, piece):
        cols = w_cols(piece)
        return remote(
            wout.at[:, cols], wz.at[z, :, cols],
            wsnd.at[direction, piece], wrcv.at[direction, piece], up[0 if direction == 0 else 2],
        )

    def w_forward(direction):
        cols = w_cols(direction)
        source = (z + 3) % 4 if direction == 0 else (z + 1) % 4
        return remote(
            wz.at[source, :, cols], wz.at[source, :, cols],
            wfsnd.at[direction], wfrcv.at[direction], up[0 if direction == 0 else 2],
        )

    def w_share(r):
        source = (z + r) % 4
        return remote(
            wz.at[source, :, half_cols], wz.at[source, :, half_cols],
            wcsnd.at[r - 1], wcrcv.at[r - 1], other,
        )

    half = pl.ds(pl.multiple_of(core * 256, 256), 256)
    other_half = pl.ds(pl.multiple_of((1 - core) * 256, 256), 256)

    def a_copy(s, m):
        return remote(gs.at[m, other_half], ga.at[s, m], asnd.at[s, m], arcv.at[s, m], other)

    def b_copy(s, m, r):
        target = (y + r) % 4
        rows = pl.ds(pl.multiple_of(target * 64, 64), 64)
        return remote(
            g1.at[m, rows], gb.at[s, r - 1, m], bsnd.at[s, m, r - 1], brcv.at[s, m, r - 1], along[r - 1]
        )

    def c_copy(s, m):
        rows = pl.ds(pl.multiple_of((1 - xhi) * 32, 32), 32)
        return remote(g2.at[s, m, rows], gc.at[s, m], csnd.at[s, m], crcv.at[s, m], across)

    rows32 = pl.ds(pl.multiple_of(core * 256 + y * 64 + xhi * 32, 32), 32)
    rows64 = pl.ds(pl.multiple_of(core * 256 + y * 64, 64), 64)

    def d_copy(s, m):
        part = xg.at[s, m, rows32]
        return remote(part, part, dsnd.at[s, m], drcv.at[s, m], across)

    def e_copy(s, m, r):
        part = xg.at[s, m, rows64]
        return remote(part, part, esnd.at[s, m, r - 1], ercv.at[s, m, r - 1], along[r - 1])

    def f_copy(s, m):
        part = xg.at[s, m, half]
        return remote(part, part, fsnd.at[s, m], frcv.at[s, m], other)

    def each_matrix(body):
        def turn(i, carry):
            body((i + 2) % 3)
            return carry

        lax.fori_loop(0, 3, turn, 0)

    def keys_step(s):
        if s == 1:
            each_matrix(lambda m: a_copy(0, m).wait_send())
        kn = normed(kv[0, s].astype(F32)).astype(BF)
        first = dot_nn(kn, wb[0])
        third = dot_nn(kn, wb[1])
        sigma = jax.nn.sigmoid(first)
        silu = first * sigma
        hidden = (silu * third).astype(BF)
        pull = (-rates[s] * kv[1, s].astype(F32)).astype(BF)
        gs[2] = dot_tn(hidden, pull).astype(BF)
        a_copy(s, 2).start()
        back = dot_nt(pull, wb[2])
        d_first = (back * third * sigma * (1.0 + first * (1.0 - sigma))).astype(BF)
        gs[0] = dot_tn(kn, d_first).astype(BF)
        a_copy(s, 0).start()
        d_third = (back * silu).astype(BF)
        gs[1] = dot_tn(kn, d_third).astype(BF)
        a_copy(s, 1).start()

    def queries_step(s):
        qn = normed(qv[s].astype(F32)).astype(BF)
        first = dot_nn(qn, wb[0])
        third = dot_nn(qn, wb[1])
        hidden = (first * jax.nn.sigmoid(first) * third).astype(BF)
        fo[s] = normed(dot_nn(hidden, wb[2])) * gain[...]

    def stage_b(s):
        def body(m):
            if s == 1:
                for r in (1, 2, 3):
                    b_copy(0, m, r).wait_send()
            a_copy(s, m).wait_recv()
            g1[m] = (gs[m, half].astype(F32) + ga[s, m].astype(F32)).astype(BF)
            for r in (2, 1, 3):
                b_copy(s, m, r).start()

        each_matrix(body)

    def stage_c(s):
        def body(m):
            for r in (1, 2, 3):
                b_copy(s, m, r).wait_recv()
            mine = pl.ds(pl.multiple_of(y * 64, 64), 64)
            total = g1[m, mine].astype(F32)
            for r in (1, 2, 3):
                total = total + gb[s, r - 1, m].astype(F32)
            g2[s, m] = total.astype(BF)
            c_copy(s, m).start()

        each_matrix(body)

    def stage_d(s):
        def body(m):
            c_copy(s, m).wait_recv()
            mine = pl.ds(pl.multiple_of(xhi * 32, 32), 32)
            xg[s, m, rows32] = (g2[s, m, mine].astype(F32) + gc[s, m].astype(F32)).astype(BF)
            d_copy(s, m).start()

        each_matrix(body)

    def stage_e(s):
        def body(m):
            d_copy(s, m).wait_recv()
            for r in (2, 1, 3):
                e_copy(s, m, r).start()

        each_matrix(body)

    def stage_f(s):
        def body(m):
            for r in (1, 2, 3):
                e_copy(s, m, r).wait_recv()
            f_copy(s, m).start()

        each_matrix(body)

    def update(s):
        def body(m):
            f_copy(s, m).wait_recv()
            f_copy(s, m).wait_send()
            d_copy(s, m).wait_send()
            for r in (1, 2, 3):
                e_copy(s, m, r).wait_send()
            grad = xg[s, m].astype(F32)
            square = jnp.sum(grad * grad)
            xg[s, m] = (grad * lax.rsqrt(square + 1e-06)).astype(BF)

            def newton(turn, carry):
                ortho = xg[s, m]
                gram = dot_tn(ortho, ortho).astype(BF)
                poly = (coef_b * gram.astype(F32) + coef_c * dot_nn(gram, gram)).astype(BF)
                moved = dot_nn(ortho, poly)
                xg[s, m] = (coef_a * ortho.astype(F32) + moved).astype(BF)
                return carry

            lax.fori_loop(0, NS_ITERS, newton, 0)
            old = state[m]
            fresh = old - xg[s, m].astype(F32)
            target = jnp.mean(old * old, axis=-1, keepdims=True) + 1e-06
            actual = jnp.mean(fresh * fresh, axis=-1, keepdims=True) + 1e-06
            new = fresh * (jnp.sqrt(target) * lax.rsqrt(actual))
            state[m] = new
            wb[m] = new.astype(BF)

        each_matrix(body)

    scale = AH ** (-0.5)

    def attend(d, s):
        def tile(hd, carry):
            cols = pl.ds(pl.multiple_of(hd * AH, AH), AH)
            i = s * 4 + hd
            q = qv[s, :, cols]
            if d == 0:
                k, v = kv[0, s, :, cols], kv[1, s, :, cols]
            else:
                src = s - (ctx < d).astype(jnp.int32) if s else 0
                k, v = win[d - 1, 0, src, :, cols], win[d - 1, 1, src, :, cols]
            scores = dot_nt(q, k) * scale
            if d in (0, 4):
                row = lax.broadcasted_iota(jnp.int32, scores.shape, 0)
                col = lax.broadcasted_iota(jnp.int32, scores.shape, 1)
                scores = jnp.where(col <= row if d == 0 else col > row, scores, -1e30)
            top = jnp.max(scores, axis=-1, keepdims=True)
            if d == 0:
                probs = jnp.exp(scores - top)
                mrow[i] = top
                lrow[i] = jnp.sum(probs, axis=-1, keepdims=True)
                acc[s, :, cols] = dot_nn(probs.astype(BF), v)
            else:
                before = mrow[i]
                top = jnp.maximum(before, top)
                probs = jnp.exp(scores - top)
                keep = jnp.exp(before - top)
                mrow[i] = top
                lrow[i] = lrow[i] * keep + jnp.sum(probs, axis=-1, keepdims=True)
                acc[s, :, cols] = acc[s, :, cols] * keep + dot_nn(probs.astype(BF), v)
            return carry

        def run():
            lax.fori_loop(0, 4, tile, 0)

        if d and s == 0:
            pl.when(ctx >= d)(run)
        else:
            run()

    def mix(s):
        for hd in range(4):
            cols = slice(hd * AH, (hd + 1) * AH)
            attn = acc[s, :, cols] * (1.0 / lrow[s * 4 + hd])
            mixed[s, :, cols] = (fo[s, :, cols] + attn).astype(BF)

    def z_copy(s, r, part):
        target = (z + r) % 4
        rows = pl.ds(pl.multiple_of((part * 4 + target) * 64, 64), 64)
        return remote(
            mixed.at[s, rows], mz.at[s, z, pl.ds(part * 64, 64)],
            zsnd.at[s, r - 1, part], zrcv.at[s, r - 1, part], up[r - 1],
        )

    def spread(s):
        for r in (2, 1, 3):
            for part in (0, 1):
                z_copy(s, r, part).start()
        for part in (0, 1):
            rows = pl.ds(pl.multiple_of((part * 4 + z) * 64, 64), 64)
            mz[s, z, pl.ds(part * 64, 64)] = mixed[s, rows]

    mine = pl.ds(pl.multiple_of(xlo * 64, 64), 64)
    theirs = pl.ds(pl.multiple_of((1 - xlo) * 64, 64), 64)

    def o_copy(s, piece):
        cols = pl.ds(piece * 2048, 2048)
        return remote(pp.at[s, theirs, cols], pr.at[s, :, cols], osnd.at[s, piece], orcv.at[s, piece], beside)

    def project(s):
        for r in (1, 2, 3):
            for part in (0, 1):
                z_copy(s, r, part).wait_recv()
        for piece in (0, 1):
            def block(j, carry):
                cols = pl.ds(pl.multiple_of(piece * 2048 + j * 512, 512), 512)
                total = dot_nn(mz[s, 0], wz[0, :, cols])
                for zs in (1, 2, 3):
                    total = total + dot_nn(mz[s, zs], wz[zs, :, cols])
                pp[s, :, cols] = total.astype(BF)
                return carry

            lax.fori_loop(0, 4, block, 0)
            o_copy(s, piece).start()

    def finish(s):
        for piece in (0, 1):
            o_copy(s, piece).wait_recv()
            cols = pl.ds(piece * 2048, 2048)
            out[s, :, cols] = (pp[s, mine, cols].astype(F32) + pr[s, :, cols].astype(F32)).astype(BF)

    @pl.when(core == 0)
    def _():
        for i in range(4):
            c1_copy(i, False).start()

    y_copy(0).start()
    x_own(0)
    for piece in (0, 1):
        w_copy(0, piece).start()
        w_copy(1, 1 - piece).start()
    loads[4].start()
    for load in loads[:3]:
        load.wait()
    for m in range(3):
        wb[m] = state[m].astype(BF)
    keys_step(0)
    loads[3].wait()
    stage_b(0)
    y_copy(1).start()
    x_own(1)
    queries_step(0)
    attend(0, 0)
    stage_c(0)
    got_y(0)
    stage_d(0)
    attend(0, 1)
    stage_e(0)
    y_copy(2).start()
    x_own(2)
    got_y(1)
    got_x(0)
    attend(4, 0)
    stage_f(0)
    update(0)
    keys_step(1)
    stage_b(1)
    y_copy(3).start()
    x_own(3)
    queries_step(1)
    got_x(1)
    attend(2, 0)
    stage_c(1)
    got_y(2)
    w_copy(0, 0).wait_recv()
    w_forward(0).start()
    w_copy(1, 1).wait_recv()
    w_forward(1).start()
    for i in (0, 1):
        c1_copy(i, False).wait_recv()
        c3_copy(i, 1).wait_recv()
    stage_d(1)
    attend(1, 0)
    attend(3, 0)
    mix(0)
    stage_e(1)
    spread(0)
    got_y(3)
    got_x(2)
    attend(4, 1)
    stage_f(1)
    w_copy(0, 1).wait_recv()
    w_share(3).start()
    w_copy(1, 0).wait_recv()
    w_share(1).start()
    got_x(3)
    attend(2, 1)
    for i in (2, 3):
        c1_copy(i, False).wait_recv()
        c3_copy(i, 1).wait_recv()
    attend(1, 1)
    attend(3, 1)
    mix(1)
    spread(1)
    w_forward(0).wait_recv()
    w_forward(1).wait_recv()
    w_share(2).start()
    update(1)
    result = pltpu.make_async_copy(state, fin, load_sem.at[5])
    result.start()
    loads[4].wait()
    for r in (1, 2, 3):
        w_share(r).wait_recv()
    project(0)
    project(1)
    finish(0)
    finish(1)
    result.wait()

    for i in range(4):
        y_copy(i).wait_send()
        x_copy(i, False).wait_send()
        c1_copy(i, False).wait_send()
        c3_copy(i, 1).wait_send()
    for direction in (0, 1):
        for piece in (0, 1):
            w_copy(direction, piece).wait_send()
        w_forward(direction).wait_send()
    for r in (1, 2, 3):
        w_share(r).wait_send()

    def drain(m):
        a_copy(1, m).wait_send()
        for r in (1, 2, 3):
            b_copy(1, m, r).wait_send()
        for s in (0, 1):
            c_copy(s, m).wait_send()

    each_matrix(drain)
    for s in (0, 1):
        for part in (0, 1):
            for r in (1, 2, 3):
                z_copy(s, r, part).wait_send()
            o_copy(s, part).wait_send()


def shards(queries, keys, values, token_rates, fast_init, out_gain, out_weight):
    dma = pltpu.SemaphoreType.DMA
    anywhere = pl.BlockSpec(memory_space=pl.ANY)
    vmem = pl.BlockSpec(memory_space=pltpu.VMEM)
    layer, final = pl.pallas_call(
        kernel,
        out_shape=(
            jax.ShapeDtypeStruct((2, 64, 4096), BF),
            jax.ShapeDtypeStruct((3, 512, 512), F32),
        ),
        in_specs=[anywhere, anywhere, anywhere, vmem, anywhere, vmem, anywhere],
        out_specs=(vmem, anywhere),
        scratch_shapes=[
            pltpu.VMEM((2, 512, 512), BF),
            pltpu.VMEM((2, 2, 512, 512), BF),
            pltpu.VMEM((4, 2, 2, 512, 512), BF),
            pltpu.VMEM((3, 512, 512), F32),
            pltpu.VMEM((3, 512, 512), BF),
            pltpu.VMEM((3, 512, 512), BF),
            pltpu.VMEM((2, 3, 256, 512), BF),
            pltpu.VMEM((3, 256, 512), BF),
            pltpu.VMEM((2, 3, 3, 64, 512), BF),
            pltpu.VMEM((2, 3, 64, 512), BF),
            pltpu.VMEM((2, 3, 32, 512), BF),
            pltpu.VMEM((2, 3, 512, 512), BF),
            pltpu.VMEM((2, 512, 512), F32),
            pltpu.VMEM((8, 512, 1), F32),
            pltpu.VMEM((8, 512, 1), F32),
            pltpu.VMEM((2, 512, 512), F32),
            pltpu.VMEM((2, 512, 512), BF),
            pltpu.VMEM((2, 4, 128, 512), BF),
            pltpu.VMEM((4, 512, 4096), BF),
            pltpu.VMEM((2, 128, 4096), BF),
            pltpu.VMEM((2, 64, 4096), BF),
            dma((6,)),
            dma((4,)), dma((4,)), dma((4,)), dma((4,)),
            dma((4,)), dma((4,)), dma((4,)), dma((4,)),
            dma((2, 3)), dma((2, 3)),
            dma((2, 3, 3)), dma((2, 3, 3)),
            dma((2, 3)), dma((2, 3)),
            dma((2, 3)), dma((2, 3)),
            dma((2, 3, 3)), dma((2, 3, 3)),
            dma((2, 3)), dma((2, 3)),
            dma((2, 2)), dma((2, 2)),
            dma((2,)), dma((2,)),
            dma((3,)), dma((3,)),
            dma((2, 3, 2)), dma((2, 3, 2)),
            dma((2, 2)), dma((2, 2)),
        ],
        compiler_params=pltpu.CompilerParams(
            collective_id=0, has_side_effects=True, vmem_limit_bytes=67000000
        ),
    )(
        queries, keys, values, token_rates, fast_init.reshape(3, 512, 512),
        out_gain.reshape(1, 512), out_weight,
    )
    return layer, final.reshape(3, 1, 512, 512)


def solution(mesh):
    placed = (
        P(None, "ctx", "head"),
        P(None, "ctx", "head"),
        P(None, "ctx", "head"),
        P(None, "ctx", "head"),
        P(None, "head", None, None),
        P("head"),
        P("head", None),
    )
    return jax.shard_map(
        shards,
        mesh=mesh,
        in_specs=placed,
        out_specs=(P(None, ("ctx", "head"), None), P(None, "head", None, None)),
        check_vma=False,
    )
```

profile of v0, /device:TPU:6, one launch (start us, length us, event | category | flops | bytes accessed | tf_op | source)
XLA Modules:
  0.0 171.7 jit_solution(9414236013220190195)
XLA Ops:
  0.6 1.7 copy.9.rates
  2.3 163.2 %shard_map.86 = (bf16[2,64,4096]{2,1,0:T(8,128)(2,1)}, f32[3,512,512]{2,1,0:T(8,128)}) custom-call(bf16[2,512,512]{2,1,0:T(8,128)(2,1)} %q_hbm.1, bf16[2,512,512]{2,1,0:T(8,128)(2,1)} %k_hbm.1, bf16[2,512,512]{2,1,0:T(8,128)(2,1)} %v_hbm.1, f32[2,512,1]{2,1,0:T(8,128)} %copy.9.rates, f32[3,512,512]{2,1,0:T(8,128)} %bitcast.6, f32[1,512]{1,0:T(1,128)} %bitcast.7, ...), custom_call_target="tpu_custom_call" | custom-call | tf_op jit(solution)/shard_map/pallas_call | solution.py:506
  165.6 2.3 %copy.13 = bf16[2,64,4096]{2,1,0:T(8,128)(2,1)} copy(bf16[2,64,4096]{2,1,0:T(8,128)(2,1)} %get-tuple-element.10) | data formatting | bytes 2097152
  167.8 3.9 %copy.14 = f32[3,1,512,512]{3,2,1,0:T(8,128)} copy(f32[3,1,512,512]{3,2,1,0:T(8,128)} %bitcast.5) | data formatting | bytes 6291456
where the time goes:
time: 174 us; the launch traced here: 172 us
  Pallas kernels  163 us (94%)
  local copies, waits for them, and re-layouts  7.85 us (5%)
    pallas_call x1, Pallas kernels, shards(): pl.pallas_call(kernel, out_shape=(jax.ShapeDtypeStruct((2, 64, 4096), BF)...  163 us
    unnamed x3, local copies, waits for them, and re-layouts  7.85 us

commit v1 on v0

--- a/solution.py
+++ b/solution.py
@@ -35,7 +35,7 @@
 def kernel(
     q_hbm, k_hbm, v_hbm, rates, w_hbm, gain, wout,
     out, fin,
-    qv, kv, win, state, wb, gs, ga, g1, gb, g2, gc, xg, acc, mrow, lrow, fo, mixed, mz, wz, pp, pr,
+    qv, kv, win, state, wb, gs, ga, g1, gb, g2, gc, xg, fo, mixed, mz, wz, pp, pr,
     load_sem, ysnd, yrcv, xsnd, xrcv, c1snd, c1rcv, c3snd, c3rcv,
     asnd, arcv, bsnd, brcv, csnd, crcv, dsnd, drcv, esnd, ercv, fsnd, frcv,
     wsnd, wrcv, wfsnd, wfrcv, wcsnd, wcrcv, zsnd, zrcv, osnd, orcv,
@@ -263,7 +263,7 @@
         each_matrix(body)
 
     def update(s):
-        def body(m):
+        for m in (2, 0, 1):
             f_copy(s, m).wait_recv()
             f_copy(s, m).wait_send()
             d_copy(s, m).wait_send()
@@ -273,71 +273,74 @@
             square = jnp.sum(grad * grad)
             xg[s, m] = (grad * lax.rsqrt(square + 1e-06)).astype(BF)
 
-            def newton(turn, carry):
-                ortho = xg[s, m]
-                gram = dot_tn(ortho, ortho).astype(BF)
-                poly = (coef_b * gram.astype(F32) + coef_c * dot_nn(gram, gram)).astype(BF)
-                moved = dot_nn(ortho, poly)
-                xg[s, m] = (coef_a * ortho.astype(F32) + moved).astype(BF)
-                return carry
-
-            lax.fori_loop(0, NS_ITERS, newton, 0)
+        def newton(turn, carry):
+            ortho = [xg[s, m] for m in range(3)]
+            gram = [dot_tn(x, x).astype(BF) for x in ortho]
+            poly = [(coef_b * g.astype(F32) + coef_c * dot_nn(g, g)).astype(BF) for g in gram]
+            for m in range(3):
+                moved = dot_nn(ortho[m], poly[m])
+                xg[s, m] = (coef_a * ortho[m].astype(F32) + moved).astype(BF)
+            return carry
+
+        lax.fori_loop(0, NS_ITERS, newton, 0)
+        for m in range(3):
             old = state[m]
             fresh = old - xg[s, m].astype(F32)
             target = jnp.mean(old * old, axis=-1, keepdims=True) + 1e-06
             actual = jnp.mean(fresh * fresh, axis=-1, keepdims=True) + 1e-06
             new = fresh * (jnp.sqrt(target) * lax.rsqrt(actual))
             state[m] = new
-            wb[m] = new.astype(BF)
-
-        each_matrix(body)
-
-    scale = AH ** (-0.5)
-
-    def attend(d, s):
-        def tile(hd, carry):
+            if s == 0:
+                wb[m] = new.astype(BF)
+
+    scale = AH ** (-0.5) * 1.4426950408889634
+
+    def attend(s):
+        lower = lax.broadcasted_iota(jnp.int32, (256, 256), 1) <= lax.broadcasted_iota(
+            jnp.int32, (256, 256), 0
+        )
+
+        def one_head(hd, carry):
             cols = pl.ds(pl.multiple_of(hd * AH, AH), AH)
-            i = s * 4 + hd
-            q = qv[s, :, cols]
-            if d == 0:
-                k, v = kv[0, s, :, cols], kv[1, s, :, cols]
-            else:
+
+            def taken(d, w, part):
+                if d == 0:
+                    return kv[w, s, part, cols]
                 src = s - (ctx < d).astype(jnp.int32) if s else 0
-                k, v = win[d - 1, 0, src, :, cols], win[d - 1, 1, src, :, cols]
-            scores = dot_nt(q, k) * scale
-            if d in (0, 4):
-                row = lax.broadcasted_iota(jnp.int32, scores.shape, 0)
-                col = lax.broadcasted_iota(jnp.int32, scores.shape, 1)
-                scores = jnp.where(col <= row if d == 0 else col > row, scores, -1e30)
-            top = jnp.max(scores, axis=-1, keepdims=True)
-            if d == 0:
-                probs = jnp.exp(scores - top)
-                mrow[i] = top
-                lrow[i] = jnp.sum(probs, axis=-1, keepdims=True)
-                acc[s, :, cols] = dot_nn(probs.astype(BF), v)
-            else:
-                before = mrow[i]
-                top = jnp.maximum(before, top)
-                probs = jnp.exp(scores - top)
-                keep = jnp.exp(before - top)
-                mrow[i] = top
-                lrow[i] = lrow[i] * keep + jnp.sum(probs, axis=-1, keepdims=True)
-                acc[s, :, cols] = acc[s, :, cols] * keep + dot_nn(probs.astype(BF), v)
+                return win[d - 1, w, src, part, cols]
+
+            def values(d, part):
+                v = taken(d, 1, part)
+                return jnp.concatenate([v, jnp.ones_like(v)], axis=1)
+
+            low, high, whole = pl.ds(0, 256), pl.ds(256, 256), pl.ds(0, 512)
+            for block in (0, 1):
+                here = (low, high)[block]
+                q = qv[s, here, cols]
+
+                def scores(d, part):
+                    x = dot_nt(q, taken(d, 0, part)) * scale
+                    if s == 0 and d:
+                        x = x + jnp.where(ctx < d, -1e30, 0.0)
+                    return x
+
+                side = (4, high) if block == 0 else (0, low)
+                parts = [(1, whole), (2, whole), (3, whole), side]
+                near, far = scores(0, here), scores(4, here)
+                logits = [jnp.where(lower, near, far)] + [scores(d, part) for d, part in parts]
+                top = jnp.max(logits[0], axis=-1, keepdims=True)
+                for x in logits[1:]:
+                    top = jnp.maximum(top, jnp.max(x, axis=-1, keepdims=True))
+                mid = jnp.exp2(logits[0] - top)
+                total = dot_nn(jnp.where(lower, mid, 0.0).astype(BF), values(0, here))
+                total = total + dot_nn(jnp.where(lower, 0.0, mid).astype(BF), values(4, here))
+                for x, (d, part) in zip(logits[1:], parts):
+                    total = total + dot_nn(jnp.exp2(x - top).astype(BF), values(d, part))
+                attn = total[:, :AH] / total[:, AH:]
+                mixed[s, here, cols] = (fo[s, here, cols] + attn).astype(BF)
             return carry
 
-        def run():
-            lax.fori_loop(0, 4, tile, 0)
-
-        if d and s == 0:
-            pl.when(ctx >= d)(run)
-        else:
-            run()
-
-    def mix(s):
-        for hd in range(4):
-            cols = slice(hd * AH, (hd + 1) * AH)
-            attn = acc[s, :, cols] * (1.0 / lrow[s * 4 + hd])
-            mixed[s, :, cols] = (fo[s, :, cols] + attn).astype(BF)
+        lax.fori_loop(0, 4, one_head, 0)
 
     def z_copy(s, r, part):
         target = (z + r) % 4
@@ -359,38 +362,42 @@
     theirs = pl.ds(pl.multiple_of((1 - xlo) * 64, 64), 64)
 
     def o_copy(s, piece):
-        cols = pl.ds(piece * 2048, 2048)
+        cols = pl.ds(pl.multiple_of(piece * 1024, 1024), 1024)
         return remote(pp.at[s, theirs, cols], pr.at[s, :, cols], osnd.at[s, piece], orcv.at[s, piece], beside)
 
     def project(s):
         for r in (1, 2, 3):
             for part in (0, 1):
                 z_copy(s, r, part).wait_recv()
-        for piece in (0, 1):
-            def block(j, carry):
-                cols = pl.ds(pl.multiple_of(piece * 2048 + j * 512, 512), 512)
-                total = dot_nn(mz[s, 0], wz[0, :, cols])
-                for zs in (1, 2, 3):
-                    total = total + dot_nn(mz[s, zs], wz[zs, :, cols])
-                pp[s, :, cols] = total.astype(BF)
-                return carry
-
-            lax.fori_loop(0, 4, block, 0)
+        def block(piece, carry):
+            cols = pl.ds(pl.multiple_of(piece * 1024, 1024), 1024)
+            total = dot_nn(mz[s, 0], wz[0, :, cols])
+            for zs in (1, 2, 3):
+                total = total + dot_nn(mz[s, zs], wz[zs, :, cols])
+            pp[s, :, cols] = total.astype(BF)
             o_copy(s, piece).start()
+            return carry
+
+        lax.fori_loop(0, 4, block, 0)
 
     def finish(s):
-        for piece in (0, 1):
+        for piece in range(4):
             o_copy(s, piece).wait_recv()
-            cols = pl.ds(piece * 2048, 2048)
+            cols = pl.ds(piece * 1024, 1024)
             out[s, :, cols] = (pp[s, mine, cols].astype(F32) + pr[s, :, cols].astype(F32)).astype(BF)
 
-    @pl.when(core == 0)
-    def _():
-        for i in range(4):
+    def near_own(i):
+        @pl.when(core == 0)
+        def _():
             c1_copy(i, False).start()
+
+    def got_near(i):
+        c1_copy(i, False).wait_recv()
+        c3_copy(i, 1).wait_recv()
 
     y_copy(0).start()
     x_own(0)
+    x_own(1)
     for piece in (0, 1):
         w_copy(0, piece).start()
         w_copy(1, 1 - piece).start()
@@ -403,70 +410,61 @@
     loads[3].wait()
     stage_b(0)
     y_copy(1).start()
-    x_own(1)
+    x_own(2)
+    near_own(0)
+    near_own(1)
     queries_step(0)
-    attend(0, 0)
     stage_c(0)
     got_y(0)
     stage_d(0)
-    attend(0, 1)
+    x_own(3)
     stage_e(0)
     y_copy(2).start()
-    x_own(2)
+    y_copy(3).start()
     got_y(1)
     got_x(0)
-    attend(4, 0)
-    stage_f(0)
-    update(0)
-    keys_step(1)
-    stage_b(1)
-    y_copy(3).start()
-    x_own(3)
-    queries_step(1)
-    got_x(1)
-    attend(2, 0)
-    stage_c(1)
-    got_y(2)
     w_copy(0, 0).wait_recv()
     w_forward(0).start()
     w_copy(1, 1).wait_recv()
     w_forward(1).start()
-    for i in (0, 1):
-        c1_copy(i, False).wait_recv()
-        c3_copy(i, 1).wait_recv()
+    stage_f(0)
+    near_own(2)
+    near_own(3)
+    update(0)
+    keys_step(1)
+    got_x(1)
+    stage_b(1)
+    got_y(2)
+    queries_step(1)
+    got_near(0)
+    got_near(1)
+    attend(0)
+    spread(0)
+    stage_c(1)
+    got_x(2)
+    got_y(3)
     stage_d(1)
-    attend(1, 0)
-    attend(3, 0)
-    mix(0)
-    stage_e(1)
-    spread(0)
-    got_y(3)
-    got_x(2)
-    attend(4, 1)
-    stage_f(1)
     w_copy(0, 1).wait_recv()
     w_share(3).start()
     w_copy(1, 0).wait_recv()
     w_share(1).start()
+    stage_e(1)
     got_x(3)
-    attend(2, 1)
-    for i in (2, 3):
-        c1_copy(i, False).wait_recv()
-        c3_copy(i, 1).wait_recv()
-    attend(1, 1)
-    attend(3, 1)
-    mix(1)
+    got_near(2)
+    got_near(3)
+    attend(1)
     spread(1)
+    stage_f(1)
     w_forward(0).wait_recv()
     w_forward(1).wait_recv()
     w_share(2).start()
-    update(1)
-    result = pltpu.make_async_copy(state, fin, load_sem.at[5])
-    result.start()
     loads[4].wait()
     for r in (1, 2, 3):
         w_share(r).wait_recv()
     project(0)
+    update(1)
+    result = pltpu.make_async_copy(state, fin, load_sem.at[5])
+    result.start()
     project(1)
     finish(0)
     finish(1)
@@ -496,7 +494,8 @@
         for part in (0, 1):
             for r in (1, 2, 3):
                 z_copy(s, r, part).wait_send()
-            o_copy(s, part).wait_send()
+        for piece in range(4):
+            o_copy(s, piece).wait_send()
 
 
 def shards(queries, keys, values, token_rates, fast_init, out_gain, out_weight):
@@ -525,9 +524,6 @@
             pltpu.VMEM((2, 3, 32, 512), BF),
             pltpu.VMEM((2, 3, 512, 512), BF),
             pltpu.VMEM((2, 512, 512), F32),
-            pltpu.VMEM((8, 512, 1), F32),
-            pltpu.VMEM((8, 512, 1), F32),
-            pltpu.VMEM((2, 512, 512), F32),
             pltpu.VMEM((2, 512, 512), BF),
             pltpu.VMEM((2, 4, 128, 512), BF),
             pltpu.VMEM((4, 512, 4096), BF),
@@ -546,7 +542,7 @@
             dma((2,)), dma((2,)),
             dma((3,)), dma((3,)),
             dma((2, 3, 2)), dma((2, 3, 2)),
-            dma((2, 2)), dma((2, 2)),
+            dma((2, 4)), dma((2, 4)),
         ],
         compiler_params=pltpu.CompilerParams(
             collective_id=0, has_side_effects=True, vmem_limit_bytes=67000000

time: 174 us -> 152 us (0.87)
  the two profiles are of different devices: /device:TPU:6 before, /device:TPU:0 now
where the time goes in v1:
time: 152 us
  Pallas kernels  144 us (95%)
  local copies, waits for them, and re-layouts  7.85 us (5%)
    pallas_call x1, Pallas kernels, shards(): pl.pallas_call(kernel, out_shape=(jax.ShapeDtypeStruct((2, 64, 4096), BF)...  144 us
    unnamed x3, local copies, waits for them, and re-layouts  7.85 us

profile of v1, /device:TPU:0, one launch (start us, length us, event | category | flops | bytes accessed | tf_op | source)
XLA Modules:
  0.0 152.1 jit_solution(9978543235992009609)
XLA Ops:
  0.6 1.7 %copy.9.rates = f32[2,512,1]{2,1,0:T(8,128)} copy(f32[2,512,1]{1,2,0:T(1,128)} %param.10) | data formatting | bytes 8192 | tf_op args[3]
  2.3 143.6 %shard_map.86 = (bf16[2,64,4096]{2,1,0:T(8,128)(2,1)}, f32[3,512,512]{2,1,0:T(8,128)}) custom-call(bf16[2,512,512]{2,1,0:T(8,128)(2,1)} %q_hbm.1, bf16[2,512,512]{2,1,0:T(8,128)(2,1)} %k_hbm.1, bf16[2,512,512]{2,1,0:T(8,128)(2,1)} %v_hbm.1, f32[2,512,1]{2,1,0:T(8,128)} %copy.9.rates, f32[3,512,512]{2,1,0:T(8,128)} %bitcast.6, f32[1,512]{1,0:T(1,128)} %bitcast.7, ...), custom_call_target="tpu_custom_call" | custom-call | tf_op jit(solution)/shard_map/pallas_call | solution.py:505
  146.0 2.3 %copy.13 = bf16[2,64,4096]{2,1,0:T(8,128)(2,1)} copy(bf16[2,64,4096]{2,1,0:T(8,128)(2,1)} %get-tuple-element.10) | data formatting | bytes 2097152
  148.3 3.9 %copy.14 = f32[3,1,512,512]{3,2,1,0:T(8,128)} copy(f32[3,1,512,512]{3,2,1,0:T(8,128)} %bitcast.5) | data formatting | bytes 6291456

commit v2 on v1

--- a/solution.py
+++ b/solution.py
@@ -194,7 +194,8 @@
         sigma = jax.nn.sigmoid(first)
         silu = first * sigma
         hidden = (silu * third).astype(BF)
-        pull = (-rates[s] * kv[1, s].astype(F32)).astype(BF)
+        rate = jnp.transpose(jnp.broadcast_to(rates[s], (128, 512)))
+        pull = (-jnp.concatenate([rate] * 4, axis=1) * kv[1, s].astype(F32)).astype(BF)
         gs[2] = dot_tn(hidden, pull).astype(BF)
         a_copy(s, 2).start()
         back = dot_nt(pull, wb[2])
@@ -295,7 +296,7 @@
 
     scale = AH ** (-0.5) * 1.4426950408889634
 
-    def attend(s):
+    def attend(s, block):
         lower = lax.broadcasted_iota(jnp.int32, (256, 256), 1) <= lax.broadcasted_iota(
             jnp.int32, (256, 256), 0
         )
@@ -314,7 +315,7 @@
                 return jnp.concatenate([v, jnp.ones_like(v)], axis=1)
 
             low, high, whole = pl.ds(0, 256), pl.ds(256, 256), pl.ds(0, 512)
-            for block in (0, 1):
+            if True:
                 here = (low, high)[block]
                 q = qv[s, here, cols]
 
@@ -346,17 +347,25 @@
         target = (z + r) % 4
         rows = pl.ds(pl.multiple_of((part * 4 + target) * 64, 64), 64)
         return remote(
-            mixed.at[s, rows], mz.at[s, z, pl.ds(part * 64, 64)],
+            mixed.at[s, rows], mz.at[s, z, pl.ds(pl.multiple_of(part * 64, 64), 64)],
             zsnd.at[s, r - 1, part], zrcv.at[s, r - 1, part], up[r - 1],
         )
 
-    def spread(s):
+    def spread(s, part):
         for r in (2, 1, 3):
-            for part in (0, 1):
-                z_copy(s, r, part).start()
-        for part in (0, 1):
-            rows = pl.ds(pl.multiple_of((part * 4 + z) * 64, 64), 64)
-            mz[s, z, pl.ds(part * 64, 64)] = mixed[s, rows]
+            z_copy(s, r, part).start()
+        here = pl.ds(pl.multiple_of(part * 64, 64), 64)
+        mz[s, z, here] = mixed[s, pl.ds(pl.multiple_of((part * 4 + z) * 64, 64), 64)]
+
+    def attend_by_owner(s):
+        def turn(step, carry):
+            part = jnp.where(step == 0, 1 - xlo, xlo)
+            pl.when(part == 0)(lambda: attend(s, 0))
+            pl.when(part == 1)(lambda: attend(s, 1))
+            spread(s, part)
+            return carry
+
+        lax.fori_loop(0, 2, turn, 0)
 
     mine = pl.ds(pl.multiple_of(xlo * 64, 64), 64)
     theirs = pl.ds(pl.multiple_of((1 - xlo) * 64, 64), 64)
@@ -365,17 +374,21 @@
         cols = pl.ds(pl.multiple_of(piece * 1024, 1024), 1024)
         return remote(pp.at[s, theirs, cols], pr.at[s, :, cols], osnd.at[s, piece], orcv.at[s, piece], beside)
 
-    def project(s):
+    def project(s, part=None):
+        parts = (0, 1) if part is None else (part,)
         for r in (1, 2, 3):
-            for part in (0, 1):
-                z_copy(s, r, part).wait_recv()
+            for each in parts:
+                z_copy(s, r, each).wait_recv()
+        here = pl.ds(0, 128) if part is None else pl.ds(pl.multiple_of(part * 64, 64), 64)
+
         def block(piece, carry):
             cols = pl.ds(pl.multiple_of(piece * 1024, 1024), 1024)
-            total = dot_nn(mz[s, 0], wz[0, :, cols])
+            total = dot_nn(mz[s, 0, here], wz[0, :, cols])
             for zs in (1, 2, 3):
-                total = total + dot_nn(mz[s, zs], wz[zs, :, cols])
-            pp[s, :, cols] = total.astype(BF)
-            o_copy(s, piece).start()
+                total = total + dot_nn(mz[s, zs, here], wz[zs, :, cols])
+            pp[s, here, cols] = total.astype(BF)
+            if part is not xlo:
+                o_copy(s, piece).start()
             return carry
 
         lax.fori_loop(0, 4, block, 0)
@@ -435,37 +448,39 @@
     got_x(1)
     stage_b(1)
     got_y(2)
-    queries_step(1)
-    got_near(0)
-    got_near(1)
-    attend(0)
-    spread(0)
-    stage_c(1)
-    got_x(2)
-    got_y(3)
-    stage_d(1)
     w_copy(0, 1).wait_recv()
     w_share(3).start()
     w_copy(1, 0).wait_recv()
     w_share(1).start()
-    stage_e(1)
-    got_x(3)
-    got_near(2)
-    got_near(3)
-    attend(1)
-    spread(1)
-    stage_f(1)
+    queries_step(1)
+    got_near(0)
+    got_near(1)
+    attend(0, 0)
+    spread(0, 0)
+    got_y(3)
+    got_x(2)
+    attend(0, 1)
+    spread(0, 1)
     w_forward(0).wait_recv()
     w_forward(1).wait_recv()
     w_share(2).start()
+    stage_c(1)
     loads[4].wait()
     for r in (1, 2, 3):
         w_share(r).wait_recv()
     project(0)
+    got_x(3)
+    stage_d(1)
+    stage_e(1)
+    got_near(2)
+    got_near(3)
+    attend_by_owner(1)
+    stage_f(1)
+    project(1, 1 - xlo)
     update(1)
     result = pltpu.make_async_copy(state, fin, load_sem.at[5])
     result.start()
-    project(1)
+    project(1, xlo)
     finish(0)
     finish(1)
     result.wait()
@@ -548,7 +563,7 @@
             collective_id=0, has_side_effects=True, vmem_limit_bytes=67000000
         ),
     )(
-        queries, keys, values, token_rates, fast_init.reshape(3, 512, 512),
+        queries, keys, values, token_rates.reshape(2, 1, 512), fast_init.reshape(3, 512, 512),
         out_gain.reshape(1, 512), out_weight,
     )
     return layer, final.reshape(3, 1, 512, 512)

time: 152 us -> 148 us (0.974)
  the two profiles are of different devices: /device:TPU:0 before, /device:TPU:6 now
where the time goes in v2:
time: 148 us; the launch traced here: 147 us
  Pallas kernels  141 us (95%)
  local copies, waits for them, and re-layouts  6.15 us (4%)
    pallas_call x1, Pallas kernels, shards(): pl.pallas_call(kernel, out_shape=(jax.ShapeDtypeStruct((2, 64, 4096), BF)...  141 us
    unnamed x2, local copies, waits for them, and re-layouts  6.15 us

profile of v2, /device:TPU:6, one launch (start us, length us, event | category | flops | bytes accessed | tf_op | source)
XLA Modules:
  0.0 147.3 jit_solution(1397803008479157834)
XLA Ops:
  0.6 140.5 %shard_map.86 = (bf16[2,64,4096]{2,1,0:T(8,128)(2,1)}, f32[3,512,512]{2,1,0:T(8,128)}) custom-call(bf16[2,512,512]{2,1,0:T(8,128)(2,1)} %q_hbm.1, bf16[2,512,512]{2,1,0:T(8,128)(2,1)} %k_hbm.1, bf16[2,512,512]{2,1,0:T(8,128)(2,1)} %v_hbm.1, f32[2,1,512]{2,1,0:T(1,128)} %bitcast.8, f32[3,512,512]{2,1,0:T(8,128)} %bitcast.7, f32[1,512]{1,0:T(1,128)} %bitcast.9, ...), custom_call_target="tpu_custom_call" | custom-call | tf_op jit(solution)/shard_map/pallas_call | solution.py:520
  141.2 2.3 %copy.12 = bf16[2,64,4096]{2,1,0:T(8,128)(2,1)} copy(bf16[2,64,4096]{2,1,0:T(8,128)(2,1)} %get-tuple-element.10) | data formatting | bytes 2097152
  143.5 3.9 %copy.13 = f32[3,1,512,512]{3,2,1,0:T(8,128)} copy(f32[3,1,512,512]{3,2,1,0:T(8,128)} %bitcast.6) | data formatting | bytes 6291456

commit v3 on v2

--- a/solution.py
+++ b/solution.py
@@ -32,9 +32,15 @@
     return x * lax.rsqrt(jnp.mean(x * x, axis=-1, keepdims=True) + 1e-06)
 
 
+def renorm(old, fresh):
+    target = jnp.mean(old * old, axis=-1, keepdims=True) + 1e-06
+    actual = jnp.mean(fresh * fresh, axis=-1, keepdims=True) + 1e-06
+    return fresh * (jnp.sqrt(target) * lax.rsqrt(actual))
+
+
 def kernel(
     q_hbm, k_hbm, v_hbm, rates, w_hbm, gain, wout,
-    out, fin,
+    held, term, arrived, ortho_out,
     qv, kv, win, state, wb, gs, ga, g1, gb, g2, gc, xg, fo, mixed, mz, wz, pp, pr,
     load_sem, ysnd, yrcv, xsnd, xrcv, c1snd, c1rcv, c3snd, c3rcv,
     asnd, arcv, bsnd, brcv, csnd, crcv, dsnd, drcv, esnd, ercv, fsnd, frcv,
@@ -284,15 +290,13 @@
             return carry
 
         lax.fori_loop(0, NS_ITERS, newton, 0)
+        if s == 1:
+            return
         for m in range(3):
             old = state[m]
-            fresh = old - xg[s, m].astype(F32)
-            target = jnp.mean(old * old, axis=-1, keepdims=True) + 1e-06
-            actual = jnp.mean(fresh * fresh, axis=-1, keepdims=True) + 1e-06
-            new = fresh * (jnp.sqrt(target) * lax.rsqrt(actual))
+            new = renorm(old, old - xg[s, m].astype(F32))
             state[m] = new
-            if s == 0:
-                wb[m] = new.astype(BF)
+            wb[m] = new.astype(BF)
 
     scale = AH ** (-0.5) * 1.4426950408889634
 
@@ -301,7 +305,12 @@
             jnp.int32, (256, 256), 0
         )
 
-        def one_head(hd, carry):
+        def two_heads(turn, carry):
+            one_head(2 * turn)
+            one_head(2 * turn + 1)
+            return carry
+
+        def one_head(hd):
             cols = pl.ds(pl.multiple_of(hd * AH, AH), AH)
 
             def taken(d, w, part):
@@ -339,9 +348,8 @@
                     total = total + dot_nn(jnp.exp2(x - top).astype(BF), values(d, part))
                 attn = total[:, :AH] / total[:, AH:]
                 mixed[s, here, cols] = (fo[s, here, cols] + attn).astype(BF)
-            return carry
-
-        lax.fori_loop(0, 4, one_head, 0)
+
+        lax.fori_loop(0, 2, two_heads, 0)
 
     def z_copy(s, r, part):
         target = (z + r) % 4
@@ -387,7 +395,7 @@
             for zs in (1, 2, 3):
                 total = total + dot_nn(mz[s, zs, here], wz[zs, :, cols])
             pp[s, here, cols] = total.astype(BF)
-            if part is not xlo:
+            if part is not None and part is not xlo:
                 o_copy(s, piece).start()
             return carry
 
@@ -396,8 +404,10 @@
     def finish(s):
         for piece in range(4):
             o_copy(s, piece).wait_recv()
-            cols = pl.ds(piece * 1024, 1024)
-            out[s, :, cols] = (pp[s, mine, cols].astype(F32) + pr[s, :, cols].astype(F32)).astype(BF)
+        return [
+            pltpu.make_async_copy(pp.at[s, mine], term.at[s], load_sem.at[5 + s]),
+            pltpu.make_async_copy(pr.at[s], arrived.at[s], load_sem.at[7 + s]),
+        ]
 
     def near_own(i):
         @pl.when(core == 0)
@@ -428,8 +438,8 @@
     near_own(1)
     queries_step(0)
     stage_c(0)
+    stage_d(0)
     got_y(0)
-    stage_d(0)
     x_own(3)
     stage_e(0)
     y_copy(2).start()
@@ -444,6 +454,8 @@
     near_own(2)
     near_own(3)
     update(0)
+    kept = pltpu.make_async_copy(state, held, load_sem.at[9])
+    kept.start()
     keys_step(1)
     got_x(1)
     stage_b(1)
@@ -471,6 +483,8 @@
     project(0)
     got_x(3)
     stage_d(1)
+    for piece in range(4):
+        o_copy(0, piece).start()
     stage_e(1)
     got_near(2)
     got_near(3)
@@ -478,12 +492,14 @@
     stage_f(1)
     project(1, 1 - xlo)
     update(1)
-    result = pltpu.make_async_copy(state, fin, load_sem.at[5])
+    result = pltpu.make_async_copy(xg.at[1], ortho_out, load_sem.at[10])
     result.start()
     project(1, xlo)
-    finish(0)
-    finish(1)
-    result.wait()
+    ends = finish(0) + finish(1)
+    for end in ends:
+        end.start()
+    for end in ends + [kept, result]:
+        end.wait()
 
     for i in range(4):
         y_copy(i).wait_send()
@@ -513,18 +529,27 @@
             o_copy(s, piece).wait_send()
 
 
+def close(held, term, arrived, ortho, out, fin):
+    out[...] = (term[...].astype(F32) + arrived[...].astype(F32)).astype(BF)
+    for m in range(3):
+        old = held[m]
+        fin[m] = renorm(old, old - ortho[m].astype(F32))
+
+
 def shards(queries, keys, values, token_rates, fast_init, out_gain, out_weight):
     dma = pltpu.SemaphoreType.DMA
     anywhere = pl.BlockSpec(memory_space=pl.ANY)
     vmem = pl.BlockSpec(memory_space=pltpu.VMEM)
-    layer, final = pl.pallas_call(
+    held, term, arrived, ortho = pl.pallas_call(
         kernel,
         out_shape=(
+            jax.ShapeDtypeStruct((3, 512, 512), F32),
             jax.ShapeDtypeStruct((2, 64, 4096), BF),
-            jax.ShapeDtypeStruct((3, 512, 512), F32),
+            jax.ShapeDtypeStruct((2, 64, 4096), BF),
+            jax.ShapeDtypeStruct((3, 512, 512), BF),
         ),
         in_specs=[anywhere, anywhere, anywhere, vmem, anywhere, vmem, anywhere],
-        out_specs=(vmem, anywhere),
+        out_specs=(anywhere, anywhere, anywhere, anywhere),
         scratch_shapes=[
             pltpu.VMEM((2, 512, 512), BF),
             pltpu.VMEM((2, 2, 512, 512), BF),
@@ -544,7 +569,7 @@
             pltpu.VMEM((4, 512, 4096), BF),
             pltpu.VMEM((2, 128, 4096), BF),
             pltpu.VMEM((2, 64, 4096), BF),
-            dma((6,)),
+            dma((11,)),
             dma((4,)), dma((4,)), dma((4,)), dma((4,)),
             dma((4,)), dma((4,)), dma((4,)), dma((4,)),
             dma((2, 3)), dma((2, 3)),
@@ -566,6 +591,19 @@
         queries, keys, values, token_rates.reshape(2, 1, 512), fast_init.reshape(3, 512, 512),
         out_gain.reshape(1, 512), out_weight,
     )
+    rows = pl.BlockSpec((3, 64, 512), lambda i: (0, i, 0))
+    wide = pl.BlockSpec((2, 64, 512), lambda i: (0, 0, i))
+    layer, final = pl.pallas_call(
+        close,
+        grid=(8,),
+        out_shape=(
+            jax.ShapeDtypeStruct((2, 64, 4096), BF),
+            jax.ShapeDtypeStruct((3, 512, 512), F32),
+        ),
+        in_specs=[rows, wide, wide, rows],
+        out_specs=(wide, rows),
+        compiler_params=pltpu.CompilerParams(vmem_limit_bytes=60000000),
+    )(held, term, arrived, ortho)
     return layer, final.reshape(3, 1, 512, 512)
 
 

time: 148 us -> 137 us (0.926)
  local copies, waits for them, and re-layouts: 6.15 us -> 0 us
  Pallas kernels: 141 us -> 136 us
    unnamed x2 -> x0, local copies, waits for them, and re-layouts: 6.15 us -> none
    pallas_call x1 -> x2, Pallas kernels: 141 us -> 136 us  [the longest x1 128 us: shards(): pl.pallas_call(kernel, out_shape=(jax.ShapeDtypeStruct((3, 512, 512), F32...]
where the time goes in v3:
time: 137 us; the launch traced here: 136 us
  Pallas kernels  136 us (99%)
    pallas_call x1, Pallas kernels, shards(): pl.pallas_call(kernel, out_shape=(jax.ShapeDtypeStruct((3, 512, 512), F32...  128 us
    pallas_call x1, Pallas kernels, shards(): pl.pallas_call(close, grid=(8,), out_shape=(jax.ShapeDtypeStruct((2, 64,...  7.65 us

profile of v3, /device:TPU:6, one launch (start us, length us, event | category | flops | bytes accessed | tf_op | source)
XLA Modules:
  0.0 136.4 jit_solution(12224660742667077536)
XLA Ops:
  0.6 128.1 %shard_map.86 = (f32[3,512,512]{2,1,0:T(8,128)}, bf16[2,64,4096]{2,1,0:T(8,128)(2,1)}, bf16[2,64,4096]{2,1,0:T(8,128)(2,1)}, bf16[3,512,512]{2,1,0:T(8,128)(2,1)}) custom-call(bf16[2,512,512]{2,1,0:T(8,128)(2,1)} %q_hbm.1, bf16[2,512,512]{2,1,0:T(8,128)(2,1)} %k_hbm.1, bf16[2,512,512]{2,1,0:T(8,128)(2,1)} %v_hbm.1, f32[2,1,512]{2,1,0:T(1,128)} %bitcast.7, ...), custom_call_target="tpu_custom_call" | custom-call | tf_op jit(solution)/shard_map/pallas_call | solution.py:543
  128.7 7.7 %shard_map.87 = (bf16[2,64,4096]{2,1,0:T(8,128)(2,1)}, f32[3,512,512]{2,1,0:T(8,128)}) custom-call(f32[3,512,512]{2,1,0:T(8,128)} %get-tuple-element.8.held, bf16[2,64,4096]{2,1,0:T(8,128)(2,1)} %get-tuple-element.9.term, bf16[2,64,4096]{2,1,0:T(8,128)(2,1)} %get-tuple-element.10.arrived, bf16[3,512,512]{2,1,0:T(8,128)(2,1)} %get-tuple-element.11.ortho), custom_call_target="tpu_custom_call" | custom-call | tf_op jit(solution)/shard_map/pallas_call | solution.py:596

commit v4 on v3

--- a/solution.py
+++ b/solution.py
@@ -30,6 +30,11 @@
 
 def normed(x):
     return x * lax.rsqrt(jnp.mean(x * x, axis=-1, keepdims=True) + 1e-06)
+
+
+def mirrored(top, corner):
+    bottom = jnp.concatenate([jnp.transpose(top[:, 256:]), corner], axis=1)
+    return jnp.concatenate([top, bottom], axis=0)
 
 
 def renorm(old, fresh):
@@ -282,8 +287,19 @@
 
         def newton(turn, carry):
             ortho = [xg[s, m] for m in range(3)]
-            gram = [dot_tn(x, x).astype(BF) for x in ortho]
-            poly = [(coef_b * g.astype(F32) + coef_c * dot_nn(g, g)).astype(BF) for g in gram]
+            gram = [
+                mirrored(dot_tn(x[:, :256], x).astype(BF), dot_tn(x[:, 256:], x[:, 256:]).astype(BF))
+                for x in ortho
+            ]
+            poly = [
+                mirrored(
+                    (coef_b * g[:256].astype(F32) + coef_c * dot_nn(g[:256], g)).astype(BF),
+                    (
+                        coef_b * g[256:, 256:].astype(F32) + coef_c * dot_nn(g[256:], g[:, 256:])
+                    ).astype(BF),
+                )
+                for g in gram
+            ]
             for m in range(3):
                 moved = dot_nn(ortho[m], poly[m])
                 xg[s, m] = (coef_a * ortho[m].astype(F32) + moved).astype(BF)
@@ -365,12 +381,13 @@
         here = pl.ds(pl.multiple_of(part * 64, 64), 64)
         mz[s, z, here] = mixed[s, pl.ds(pl.multiple_of((part * 4 + z) * 64, 64), 64)]
 
-    def attend_by_owner(s):
+    def attend_by_owner(s, between):
         def turn(step, carry):
             part = jnp.where(step == 0, 1 - xlo, xlo)
             pl.when(part == 0)(lambda: attend(s, 0))
             pl.when(part == 1)(lambda: attend(s, 1))
             spread(s, part)
+            pl.when(step == 0)(between)
             return carry
 
         lax.fori_loop(0, 2, turn, 0)
@@ -477,24 +494,23 @@
     w_forward(1).wait_recv()
     w_share(2).start()
     stage_c(1)
+    got_x(3)
     loads[4].wait()
     for r in (1, 2, 3):
         w_share(r).wait_recv()
     project(0)
-    got_x(3)
     stage_d(1)
     for piece in range(4):
         o_copy(0, piece).start()
-    stage_e(1)
     got_near(2)
     got_near(3)
-    attend_by_owner(1)
+    attend_by_owner(1, lambda: stage_e(1))
+    project(1, 1 - xlo)
+    project(1, xlo)
     stage_f(1)
-    project(1, 1 - xlo)
     update(1)
     result = pltpu.make_async_copy(xg.at[1], ortho_out, load_sem.at[10])
     result.start()
-    project(1, xlo)
     ends = finish(0) + finish(1)
     for end in ends:
         end.start()
@@ -531,9 +547,8 @@
 
 def close(held, term, arrived, ortho, out, fin):
     out[...] = (term[...].astype(F32) + arrived[...].astype(F32)).astype(BF)
-    for m in range(3):
-        old = held[m]
-        fin[m] = renorm(old, old - ortho[m].astype(F32))
+    old = held[...]
+    fin[...] = renorm(old, old - ortho[...].astype(F32))
 
 
 def shards(queries, keys, values, token_rates, fast_init, out_gain, out_weight):
@@ -591,20 +606,23 @@
         queries, keys, values, token_rates.reshape(2, 1, 512), fast_init.reshape(3, 512, 512),
         out_gain.reshape(1, 512), out_weight,
     )
-    rows = pl.BlockSpec((3, 64, 512), lambda i: (0, i, 0))
-    wide = pl.BlockSpec((2, 64, 512), lambda i: (0, 0, i))
+    rows = pl.BlockSpec((384, 512), lambda i: (i, 0))
+    wide = pl.BlockSpec((32, 4096), lambda i: (i, 0))
     layer, final = pl.pallas_call(
         close,
-        grid=(8,),
+        grid=(4,),
         out_shape=(
-            jax.ShapeDtypeStruct((2, 64, 4096), BF),
-            jax.ShapeDtypeStruct((3, 512, 512), F32),
+            jax.ShapeDtypeStruct((128, 4096), BF),
+            jax.ShapeDtypeStruct((1536, 512), F32),
         ),
         in_specs=[rows, wide, wide, rows],
         out_specs=(wide, rows),
         compiler_params=pltpu.CompilerParams(vmem_limit_bytes=60000000),
-    )(held, term, arrived, ortho)
-    return layer, final.reshape(3, 1, 512, 512)
+    )(
+        held.reshape(1536, 512), term.reshape(128, 4096), arrived.reshape(128, 4096),
+        ortho.reshape(1536, 512),
+    )
+    return layer.reshape(2, 64, 4096), final.reshape(3, 1, 512, 512)
 
 
 def solution(mesh):

time: 137 us -> 134 us (0.978)
  Pallas kernels: 136 us -> 132 us
    pallas_call x1, Pallas kernels: 7.65 us -> 5.59 us  [shards(): pl.pallas_call(close, grid=(4,), out_shape=(jax.ShapeDtypeStruct((128, 40...]
    pallas_call x1, Pallas kernels: 128 us -> 126 us  [shards(): pl.pallas_call(kernel, out_shape=(jax.ShapeDtypeStruct((3, 512, 512), F32...]
where the time goes in v4:
time: 134 us; the launch traced here: 132 us
  Pallas kernels  132 us (99%)
    pallas_call x1, Pallas kernels, shards(): pl.pallas_call(kernel, out_shape=(jax.ShapeDtypeStruct((3, 512, 512), F32...  126 us
    pallas_call x1, Pallas kernels, shards(): pl.pallas_call(close, grid=(4,), out_shape=(jax.ShapeDtypeStruct((128, 40...  5.59 us

profile of v4, /device:TPU:6, one launch (start us, length us, event | category | flops | bytes accessed | tf_op | source)
XLA Modules:
  0.0 132.4 jit_solution(14273037896574839493)
XLA Ops:
  0.6 126.1 %shard_map.86 = (f32[3,512,512]{2,1,0:T(8,128)}, bf16[2,64,4096]{2,1,0:T(8,128)(2,1)}, bf16[2,64,4096]{2,1,0:T(8,128)(2,1)}, bf16[3,512,512]{2,1,0:T(8,128)(2,1)}) custom-call(bf16[2,512,512]{2,1,0:T(8,128)(2,1)} %q_hbm.1, bf16[2,512,512]{2,1,0:T(8,128)(2,1)} %k_hbm.1, bf16[2,512,512]{2,1,0:T(8,128)(2,1)} %v_hbm.1, f32[2,1,512]{2,1,0:T(1,128)} %bitcast.16, ...), custom_call_target="tpu_custom_call" | custom-call | tf_op jit(solution)/shard_map/pallas_call | solution.py:558
  126.8 5.6 %shard_map.87 = (bf16[128,4096]{1,0:T(8,128)(2,1)}, f32[1536,512]{1,0:T(8,128)}) custom-call(f32[1536,512]{1,0:T(8,128)} %bitcast.12, bf16[128,4096]{1,0:T(8,128)(2,1)} %bitcast.14, bf16[128,4096]{1,0:T(8,128)(2,1)} %bitcast.15, bf16[1536,512]{1,0:T(8,128)(2,1)} %bitcast.13), custom_call_target="tpu_custom_call" | custom-call | tf_op jit(solution)/shard_map/pallas_call | solution.py:611

commit v5 on v4

--- a/solution.py
+++ b/solution.py
@@ -412,7 +412,7 @@
             for zs in (1, 2, 3):
                 total = total + dot_nn(mz[s, zs, here], wz[zs, :, cols])
             pp[s, here, cols] = total.astype(BF)
-            if part is not None and part is not xlo:
+            if part is not xlo:
                 o_copy(s, piece).start()
             return carry
 
@@ -490,27 +490,29 @@
     got_x(2)
     attend(0, 1)
     spread(0, 1)
+    stage_c(1)
+    stage_d(1)
+    got_x(3)
+    stage_e(1)
+    got_near(2)
+    got_near(3)
     w_forward(0).wait_recv()
     w_forward(1).wait_recv()
     w_share(2).start()
-    stage_c(1)
-    got_x(3)
-    loads[4].wait()
-    for r in (1, 2, 3):
-        w_share(r).wait_recv()
-    project(0)
-    stage_d(1)
-    for piece in range(4):
-        o_copy(0, piece).start()
-    got_near(2)
-    got_near(3)
-    attend_by_owner(1, lambda: stage_e(1))
+
+    def project_first():
+        loads[4].wait()
+        for r in (1, 2, 3):
+            w_share(r).wait_recv()
+        project(0)
+
+    attend_by_owner(1, project_first)
+    stage_f(1)
     project(1, 1 - xlo)
-    project(1, xlo)
-    stage_f(1)
     update(1)
     result = pltpu.make_async_copy(xg.at[1], ortho_out, load_sem.at[10])
     result.start()
+    project(1, xlo)
     ends = finish(0) + finish(1)
     for end in ends:
         end.start()

time: 134 us -> 139 us (1.037)
  Pallas kernels: 132 us -> 137 us
    pallas_call x1, Pallas kernels: 126 us -> 131 us  [shards(): pl.pallas_call(kernel, out_shape=(jax.ShapeDtypeStruct((3, 512, 512), F32...]
where the time goes in v5:
time: 139 us; the launch traced here: 138 us
  Pallas kernels  137 us (99%)
    pallas_call x1, Pallas kernels, shards(): pl.pallas_call(kernel, out_shape=(jax.ShapeDtypeStruct((3, 512, 512), F32...  131 us
    pallas_call x1, Pallas kernels, shards(): pl.pallas_call(close, grid=(4,), out_shape=(jax.ShapeDtypeStruct((128, 40...  5.59 us

profile of v5, /device:TPU:6, one launch (start us, length us, event | category | flops | bytes accessed | tf_op | source)
XLA Modules:
  0.0 137.5 jit_solution(11375058807143899360)
XLA Ops:
  0.6 131.3 %shard_map.86 = (f32[3,512,512]{2,1,0:T(8,128)}, bf16[2,64,4096]{2,1,0:T(8,128)(2,1)}, bf16[2,64,4096]{2,1,0:T(8,128)(2,1)}, bf16[3,512,512]{2,1,0:T(8,128)(2,1)}) custom-call(bf16[2,512,512]{2,1,0:T(8,128)(2,1)} %q_hbm.1, bf16[2,512,512]{2,1,0:T(8,128)(2,1)} %k_hbm.1, bf16[2,512,512]{2,1,0:T(8,128)(2,1)} %v_hbm.1, f32[2,1,512]{2,1,0:T(1,128)} %bitcast.16, ...), custom_call_target="tpu_custom_call" | custom-call | tf_op jit(solution)/shard_map/pallas_call | solution.py:560
  131.9 5.6 %shard_map.87 = (bf16[128,4096]{1,0:T(8,128)(2,1)}, f32[1536,512]{1,0:T(8,128)}) custom-call(f32[1536,512]{1,0:T(8,128)} %bitcast.12, bf16[128,4096]{1,0:T(8,128)(2,1)} %bitcast.14, bf16[128,4096]{1,0:T(8,128)(2,1)} %bitcast.15, bf16[1536,512]{1,0:T(8,128)(2,1)} %bitcast.13), custom_call_target="tpu_custom_call" | custom-call | tf_op jit(solution)/shard_map/pallas_call | solution.py:613

commit v6 on v4

--- a/solution.py
+++ b/solution.py
@@ -437,7 +437,6 @@
 
     y_copy(0).start()
     x_own(0)
-    x_own(1)
     for piece in (0, 1):
         w_copy(0, piece).start()
         w_copy(1, 1 - piece).start()
@@ -450,17 +449,18 @@
     loads[3].wait()
     stage_b(0)
     y_copy(1).start()
-    x_own(2)
+    x_own(1)
     near_own(0)
     near_own(1)
     queries_step(0)
     stage_c(0)
     stage_d(0)
     got_y(0)
-    x_own(3)
+    x_own(2)
     stage_e(0)
     y_copy(2).start()
     y_copy(3).start()
+    x_own(3)
     got_y(1)
     got_x(0)
     w_copy(0, 0).wait_recv()

time: 134 us -> 126 us (0.940)
  Pallas kernels: 132 us -> 124 us
    pallas_call x1, Pallas kernels: 126 us -> 118 us  [shards(): pl.pallas_call(kernel, out_shape=(jax.ShapeDtypeStruct((3, 512, 512), F32...]
where the time goes in v6:
time: 126 us; the launch traced here: 124 us
  Pallas kernels  124 us (98%)
    pallas_call x1, Pallas kernels, shards(): pl.pallas_call(kernel, out_shape=(jax.ShapeDtypeStruct((3, 512, 512), F32...  118 us
    pallas_call x1, Pallas kernels, shards(): pl.pallas_call(close, grid=(4,), out_shape=(jax.ShapeDtypeStruct((128, 40...  5.59 us

profile of v6, /device:TPU:6, one launch (start us, length us, event | category | flops | bytes accessed | tf_op | source)
XLA Modules:
  0.0 124.4 jit_solution(18366355938247040582)
XLA Ops:
  0.6 118.2 %shard_map.86 = (f32[3,512,512]{2,1,0:T(8,128)}, bf16[2,64,4096]{2,1,0:T(8,128)(2,1)}, bf16[2,64,4096]{2,1,0:T(8,128)(2,1)}, bf16[3,512,512]{2,1,0:T(8,128)(2,1)}) custom-call(bf16[2,512,512]{2,1,0:T(8,128)(2,1)} %q_hbm.1, bf16[2,512,512]{2,1,0:T(8,128)(2,1)} %k_hbm.1, bf16[2,512,512]{2,1,0:T(8,128)(2,1)} %v_hbm.1, f32[2,1,512]{2,1,0:T(1,128)} %bitcast.16, ...), custom_call_target="tpu_custom_call" | custom-call | tf_op jit(solution)/shard_map/pallas_call | solution.py:558
  118.8 5.6 %shard_map.87 = (bf16[128,4096]{1,0:T(8,128)(2,1)}, f32[1536,512]{1,0:T(8,128)}) custom-call(f32[1536,512]{1,0:T(8,128)} %bitcast.12, bf16[128,4096]{1,0:T(8,128)(2,1)} %bitcast.14, bf16[128,4096]{1,0:T(8,128)(2,1)} %bitcast.15, bf16[1536,512]{1,0:T(8,128)(2,1)} %bitcast.13), custom_call_target="tpu_custom_call" | custom-call | tf_op jit(solution)/shard_map/pallas_call | solution.py:611

commit v7 on v6

--- a/solution.py
+++ b/solution.py
@@ -449,18 +449,17 @@
     loads[3].wait()
     stage_b(0)
     y_copy(1).start()
-    x_own(1)
     near_own(0)
     near_own(1)
     queries_step(0)
     stage_c(0)
     stage_d(0)
     got_y(0)
-    x_own(2)
+    x_own(1)
     stage_e(0)
     y_copy(2).start()
     y_copy(3).start()
-    x_own(3)
+    x_own(2)
     got_y(1)
     got_x(0)
     w_copy(0, 0).wait_recv()
@@ -468,6 +467,7 @@
     w_copy(1, 1).wait_recv()
     w_forward(1).start()
     stage_f(0)
+    x_own(3)
     near_own(2)
     near_own(3)
     update(0)

time: 126 us -> 126 us (level)
  no operation moved by 1% of the time
where the time goes in v7:
time: 126 us; the launch traced here: 124 us
  Pallas kernels  124 us (98%)
    pallas_call x1, Pallas kernels, shards(): pl.pallas_call(kernel, out_shape=(jax.ShapeDtypeStruct((3, 512, 512), F32...  118 us
    pallas_call x1, Pallas kernels, shards(): pl.pallas_call(close, grid=(4,), out_shape=(jax.ShapeDtypeStruct((128, 40...  5.59 us

profile of v7, /device:TPU:6, one launch (start us, length us, event | category | flops | bytes accessed | tf_op | source)
XLA Modules:
  0.0 124.4 jit_solution(16693853761122546792)
XLA Ops:
  0.6 118.2 %shard_map.86 = (f32[3,512,512]{2,1,0:T(8,128)}, bf16[2,64,4096]{2,1,0:T(8,128)(2,1)}, bf16[2,64,4096]{2,1,0:T(8,128)(2,1)}, bf16[3,512,512]{2,1,0:T(8,128)(2,1)}) custom-call(bf16[2,512,512]{2,1,0:T(8,128)(2,1)} %q_hbm.1, bf16[2,512,512]{2,1,0:T(8,128)(2,1)} %k_hbm.1, bf16[2,512,512]{2,1,0:T(8,128)(2,1)} %v_hbm.1, f32[2,1,512]{2,1,0:T(1,128)} %bitcast.16, ...), custom_call_target="tpu_custom_call" | custom-call | tf_op jit(solution)/shard_map/pallas_call | solution.py:558
  118.8 5.6 %shard_map.87 = (bf16[128,4096]{1,0:T(8,128)(2,1)}, f32[1536,512]{1,0:T(8,128)}) custom-call(f32[1536,512]{1,0:T(8,128)} %bitcast.12, bf16[128,4096]{1,0:T(8,128)(2,1)} %bitcast.14, bf16[128,4096]{1,0:T(8,128)(2,1)} %bitcast.15, bf16[1536,512]{1,0:T(8,128)(2,1)} %bitcast.13), custom_call_target="tpu_custom_call" | custom-call | tf_op jit(solution)/shard_map/pallas_call | solution.py:611
